TPU v7x, 128 devices: a whole 4x4x4 slice. The times are simulated.
128 devices in a mesh: omega: 16 (over x, y_hi, core), row: 4 (over z), col: 2 (over y_lo).
Axes of the slice: x: 4, y: 4 (y_hi: 2, y_lo: 2; y = y_hi * 2 + y_lo), z: 4, core: 2. Of those that a mesh axis runs over, the one named last changes fastest.
Arguments:
- frames: bfloat16 [2, 256, 512, 2048], P(None, 'omega', 'row', 'col'), may hold values from -6 to 6
- omega_taps: float32 [15], replicated, may hold values from 0.1 to 1
- smooth_kernel: float32 [5, 5], replicated, may hold values from 0.05 to 0.15
- spots: int32 [2, 3, 16384], P(None, None, ('omega', 'row', 'col')), may hold values from 0 to 2032, as said below
- counts: int32 [2, 128], P(None, ('omega', 'row', 'col')), may hold values from 1 to 128, as said below
Outputs:
- smoothed: bfloat16 [2, 256, 512, 2048], P(None, 'omega', 'row', 'col')
- scores: float32 [16384, 128], P(('omega', 'row', 'col'))
Inputs may be any that keep to these rules, and one draw needn't show every extreme that they name: `spots`: slot i belongs to block i div 128; its spot's frame lies in that block's frames and its whole 16 x 16 patch lies in that block's rows and columns. `counts`: some block of each slab has all 128 slots live.
All inputs are finite; a program needn't handle non-finite values.
Results may differ from a plain program's by a relative error of at most 0.0022.
Values may be sent and summed in bfloat16 or wider, within the bound.
A program may use at most 192 MiB of HBM per device.

v0:
```python
import functools

import jax
import jax.numpy as jnp
from jax import lax
from jax.experimental import pallas as pl
from jax.experimental.pallas import tpu as pltpu
from jax.sharding import PartitionSpec as P

TAPS = 15
PATCH = 16
HALF = 7
LANES = 128
MESH = pl.DeviceIdType.MESH
F32 = jnp.float32
BF16 = jnp.bfloat16


def normalize_patches(held, spots, counts, slab, windows, patches, normed, by_amount):
    n_frame, n_r, n_c = held.shape
    n_slot = normed.shape[0]
    lane = lax.broadcasted_iota(jnp.int32, (24, LANES), 1)
    group = lax.broadcasted_iota(jnp.int32, (n_slot, LANES), 1)
    slot = lax.broadcasted_iota(jnp.int32, (n_slot, 1), 0)

    def one(i, _):
        f = spots[0, slab, i] & (n_frame - 1)
        row = spots[1, slab, i] & (n_r - 1)
        col = spots[2, slab, i] & (n_c - 1)
        row_0 = jnp.minimum(row >> 3, n_r // 8 - 3) * 8
        col_0 = jnp.minimum(col >> 7, n_c // LANES - 2) * LANES
        shift = col - col_0
        window = held[f, pl.ds(row_0, 24), pl.ds(col_0, 2 * LANES)].astype(F32)
        left, right = window[:, :LANES], window[:, LANES:]
        if by_amount:
            turn = (2 * LANES - shift) & (LANES - 1)
            left = jnp.where(
                lane < LANES - shift, pltpu.roll(left, turn, 1), pltpu.roll(right, turn, 1)
            )
        else:
            left = jnp.where(shift >= LANES, right, left)
            for bit in (64, 32, 16, 8, 4, 2, 1):
                on = (shift & bit) != 0
                moved_left = pltpu.roll(left, LANES - bit, 1)
                moved_right = pltpu.roll(right, LANES - bit, 1)
                left = jnp.where(on, jnp.where(lane < LANES - bit, moved_left, moved_right), left)
                right = jnp.where(on, moved_right, right)
        at_window = (i & 7) * 24
        windows[pl.ds(at_window, 24)] = left
        patches[pl.ds(i * PATCH, PATCH)] = windows[pl.ds(at_window + (row - row_0), PATCH)]
        return 0

    lax.fori_loop(0, n_slot, one, 0, unroll=8)
    halves = []
    for half in range(2):
        total = jnp.zeros((n_slot, LANES), F32)
        for u in range(8):
            line = patches[pl.ds(half * 8 + u, n_slot, stride=PATCH)]
            line = pltpu.roll(line, PATCH * u, 1) if u else line
            total = jnp.where(
                jnp.logical_and(group >= PATCH * u, group < PATCH * (u + 1)), line, total
            )
        halves.append(total)
    values = jnp.concatenate(halves, axis=1)
    mean = jnp.mean(values, axis=1, keepdims=True)
    centered = values - mean
    spread = jnp.mean(centered * centered, axis=1, keepdims=True)
    result = centered / jnp.sqrt(spread + 1e-05)
    normed[...] = jnp.where(slot < counts[0, slab], result, 0.0).astype(BF16)


def layer_kernel(
    sizes,
    frames,
    taps,
    weights,
    spots,
    counts,
    own_0,
    own_1,
    mirror,
    ext_0,
    ext_1,
    slow_out,
    slow_in,
    rows_in,
    edge,
    strip,
    strip_in,
    side,
    bands,
    shifted_0,
    shifted_1,
    inverse,
    load_sem,
    edge_sem,
    rows_send,
    rows_recv,
    strip_send,
    strip_recv,
    slow_send,
    slow_recv,
    fast_send,
    fast_recv,
    windows,
    patches,
    normed,
    mirror_send,
    mirror_recv,
):
    n_omega, n_row, n_frame, n_r, n_c = sizes
    shifted = (shifted_0, shifted_1)
    ext = (ext_0, ext_1)
    own = (own_0, own_1)
    tiles = n_c // LANES
    o = lax.axis_index("omega")
    r = lax.axis_index("row")
    c = lax.axis_index("col")
    odd = lax.rem(o, 2)
    slow_o = o - 1 + 2 * odd
    fast_o = o + 1 - 2 * odd
    has_slow = jnp.logical_and(slow_o >= 0, slow_o < n_omega)
    has_up = r > 0
    has_down = r < n_row - 1

    def at(omega=o, row=r, col=c):
        return {"omega": omega, "row": row, "col": col}

    def slow_frame(j):
        return j + odd * (n_frame - 1 - 2 * j)

    def fast_frame(j):
        return slow_frame(n_frame - 1 - j)

    cuts = (0, 2, HALF, n_frame)
    order = [(slab, part) for slab in (1, 0) for part in range(3)]

    def stretch(part):
        start, stop = cuts[part], cuts[part + 1]
        return start + odd * (n_frame - stop - start), stop - start

    def edge_copy(slab):
        return pltpu.make_async_copy(
            frames.at[slab, :, :, pl.ds(pl.multiple_of((1 - c) * (n_c - LANES), LANES), LANES)],
            edge.at[slab],
            edge_sem.at[slab],
        )

    for slab in (1, 0):
        edge_copy(slab).start()

    def load(part, slab):
        first, count = stretch(part)
        return pltpu.make_async_copy(
            frames.at[slab, pl.ds(first, count)],
            own[slab].at[pl.ds(first, count)],
            load_sem.at[part, slab],
        )

    barrier = pltpu.get_barrier_semaphore()

    def greet(device):
        pl.semaphore_signal(barrier, inc=1, device_id=device, device_id_type=MESH)

    greet(at(omega=fast_o))
    greet(at(col=1 - c))
    greet(at(row=n_row - 1 - r, col=1 - c))

    @pl.when(has_slow)
    def _():
        greet(at(omega=slow_o))

    @pl.when(has_up)
    def _():
        greet(at(row=r - 1))
        greet(at(row=r - 1, col=1 - c))

    @pl.when(has_down)
    def _():
        greet(at(row=r + 1))
        greet(at(row=r + 1, col=1 - c))

    lane = lax.broadcasted_iota(jnp.int32, (n_r, LANES), 1)

    def pack(slab):
        edge_copy(slab).wait()

        def gather(f, packed):
            moved = pltpu.roll(edge[slab, f].astype(F32), 2 * f + 2 * (1 - c), 1)
            return jnp.where(jnp.logical_and(lane >= 2 * f, lane < 2 * f + 2), moved, packed)

        packed = lax.fori_loop(0, n_frame, gather, jnp.zeros((n_r, LANES), F32), unroll=4)
        strip[slab] = packed.astype(BF16)

    pack(1)
    pl.semaphore_wait(
        barrier,
        3
        + has_slow.astype(jnp.int32)
        + 2 * has_up.astype(jnp.int32)
        + 2 * has_down.astype(jnp.int32),
    )

    def strip_copy(which, slab):
        source, target, row = (
            (pl.ds(0, n_r), pl.ds(0, n_r), r),
            (pl.ds(0, 8), pl.ds(n_r + 8, 8), r - 1),
            (pl.ds(n_r - 8, 8), pl.ds(n_r, 8), r + 1),
        )[which]
        return pltpu.make_async_remote_copy(
            src_ref=strip.at[slab, source],
            dst_ref=strip_in.at[slab, target],
            send_sem=strip_send.at[which, slab],
            recv_sem=strip_recv.at[which, slab],
            device_id=at(row=row, col=1 - c),
            device_id_type=MESH,
        )

    def each_strip(slab, act):
        act(strip_copy(0, slab))

        @pl.when(has_up)
        def _():
            act(strip_copy(1, slab))

        @pl.when(has_down)
        def _():
            act(strip_copy(2, slab))

    def wait_strips(slab):
        strip_copy(0, slab).wait_recv()

        @pl.when(has_down)
        def _():
            strip_copy(1, slab).wait_recv()

        @pl.when(has_up)
        def _():
            strip_copy(2, slab).wait_recv()

    each_strip(1, lambda copy: copy.start())

    def rows_copy(part, slab, down):
        first, count = stretch(part)
        return pltpu.make_async_remote_copy(
            src_ref=frames.at[slab, pl.ds(first, count), pl.ds((n_r - 8) * down, 8)],
            dst_ref=rows_in.at[slab, pl.ds(first, count), pl.ds(8 * (1 - down), 8)],
            send_sem=rows_send.at[down, part, slab],
            recv_sem=rows_recv.at[1 - down, part, slab],
            device_id=at(row=r + 2 * down - 1),
            device_id_type=MESH,
        )

    for slab, part in order:

        @pl.when(has_up)
        def _():
            rows_copy(part, slab, 0).start()

        @pl.when(has_down)
        def _():
            rows_copy(part, slab, 1).start()

    for slab, part in order:
        load(part, slab).start()
    pack(0)
    each_strip(0, lambda copy: copy.start())

    @pl.when(jnp.logical_not(has_up))
    def _():
        rows_in[:, :, pl.ds(0, 8)] = jnp.zeros((2, n_frame, 8, n_c), BF16)
        strip_in[:, pl.ds(n_r, 8)] = jnp.zeros((2, 8, LANES), BF16)

    @pl.when(jnp.logical_not(has_down))
    def _():
        rows_in[:, :, pl.ds(8, 8)] = jnp.zeros((2, n_frame, 8, n_c), BF16)
        strip_in[:, pl.ds(n_r + 8, 8)] = jnp.zeros((2, 8, LANES), BF16)

    for f in range(n_frame):
        norm = jnp.zeros((8, LANES), F32)
        for t in range(TAPS):
            source = o * n_frame + (f + t - HALF)
            valid = jnp.logical_and(source >= 0, source < n_omega * n_frame)
            norm = norm + jnp.where(valid, taps[t], 0.0)
        inverse[f] = 1.0 / norm

    half = n_r // 2
    depth = half + 32
    to = lax.broadcasted_iota(jnp.int32, (half, depth), 0)
    source = lax.broadcasted_iota(jnp.int32, (half, depth), 1)
    top = jnp.where(source < half + 16, source, source - (half + 24))
    bottom = jnp.where(source < half + 16, source - 16, source - 24)
    upper = jnp.where(source < half + 24, top, n_r * 2) - to
    lower = jnp.where(
        jnp.logical_or(source < half + 16, source >= half + 24), bottom, n_r * 2
    ) - to
    for b in range(5):
        for which, distance in enumerate((upper, lower)):
            coarse = jnp.zeros((half, depth), F32)
            fine = jnp.zeros((half, depth), F32)
            for a in range(5):
                whole = jnp.full((half, depth), weights[a, b])
                rounded = whole.astype(BF16).astype(F32)
                coarse = jnp.where(distance == a - 2, rounded, coarse)
                fine = jnp.where(distance == a - 2, whole - rounded, fine)
            bands[which, b * half : (b + 1) * half] = jnp.concatenate(
                [coarse, fine], axis=1
            ).astype(BF16)

    @pl.when(jnp.logical_not(has_slow))
    def _():
        def clear(j, _):
            e = (HALF - 1 - j) + odd * (n_frame + 1 + 2 * j)
            for slab in (1, 0):
                ext[slab][e] = jnp.zeros((n_r, n_c), F32)
            return 0

        lax.fori_loop(0, HALF, clear, 0)

    def wait_rows(part, slab):
        @pl.when(has_up)
        def _():
            rows_copy(part, slab, 1).wait_recv()

        @pl.when(has_down)
        def _():
            rows_copy(part, slab, 0).wait_recv()

    narrow = lax.broadcasted_iota(jnp.int32, (8, LANES), 1)
    halo_lanes = jnp.where(c == 0, 0, LANES - 2)
    wide = lax.broadcasted_iota(jnp.int32, (16, LANES), 1)
    kept = jnp.logical_and(wide >= halo_lanes, wide < halo_lanes + 2)

    def smooth(slab, f, slot):
        shift = lax.rem(2 * LANES - 2 * f - 2 * c, LANES)
        for i in range(0, n_r + 16, 16):
            moved = pltpu.roll(strip_in[slab, i : i + 16].astype(F32), shift, 1)
            side[i : i + 16] = jnp.where(kept, moved, 0.0).astype(BF16)
        def multiply(part):
            own_rows = slice(part * (half - 16), part * (half - 16) + half + 16)
            for start in range(0, n_c, 2 * LANES):
                columns = slice(start, start + 2 * LANES)
                block = jnp.concatenate(
                    [own[slab][f, own_rows, columns], rows_in[slab, f, :, columns]], axis=0
                )
                shifted[part][:, columns] = jnp.dot(
                    bands[part],
                    jnp.concatenate([block, block], axis=0),
                    preferred_element_type=F32,
                )
            block = jnp.concatenate([side[own_rows], side[n_r : n_r + 16]], axis=0)
            shifted[part][:, n_c : n_c + LANES] = jnp.dot(
                bands[part], jnp.concatenate([block, block], axis=0), preferred_element_type=F32
            )

        def combine(part, at_row):
            def columns(tile):
                parts = []
                for b in range(5):
                    row = at_row + b * half
                    total = shifted[part][row : row + 8, tile * LANES : (tile + 1) * LANES]
                    parts.append(pltpu.roll(total, (2 - b) % LANES, 1) if b != 2 else total)
                return parts

            before = columns(tiles)
            around = before
            here = columns(0)
            to_row = slice(at_row + part * half, at_row + part * half + 8)
            for tile in range(tiles):
                after = columns(tile + 1) if tile + 1 < tiles else around
                value = (
                    here[2]
                    + jnp.where(narrow < 2, before[0], here[0])
                    + jnp.where(narrow < 1, before[1], here[1])
                    + jnp.where(narrow < LANES - 1, here[3], after[3])
                    + jnp.where(narrow < LANES - 2, here[4], after[4])
                )
                columns_of = slice(tile * LANES, (tile + 1) * LANES)
                ext[slab][f + HALF, to_row, columns_of] = value
                slow_out[slab, slot, to_row, columns_of] = value.astype(BF16)
                before, here = here, after

        multiply(0)
        multiply(1)
        for part in (0, 1):
            for at_row in range(0, half, 8):
                combine(part, at_row)

    def slow_copy(slab, j):
        return pltpu.make_async_remote_copy(
            src_ref=slow_out.at[slab, j],
            dst_ref=slow_in.at[slab, j],
            send_sem=slow_send.at[slab, j],
            recv_sem=slow_recv.at[slab, j],
            device_id=at(omega=slow_o),
            device_id_type=MESH,
        )

    def fast_copy(slab, j):
        return pltpu.make_async_remote_copy(
            src_ref=ext[slab].at[fast_frame(j) + HALF],
            dst_ref=ext[slab].at[HALF - 1 - j + odd * (n_frame + 1 + 2 * j)],
            send_sem=fast_send.at[slab, j],
            recv_sem=fast_recv.at[slab, j],
            device_id=at(omega=fast_o),
            device_id_type=MESH,
        )

    def arrive(slab, j):
        slow_copy(slab, j).wait_recv()
        e = (HALF - 1 - j) + odd * (n_frame + 1 + 2 * j)

        def widen(i, _):
            at_row = pl.multiple_of(i * 16, 16)
            ext[slab][e, pl.ds(at_row, 16)] = slow_in[slab, j, pl.ds(at_row, 16)].astype(F32)
            return 0

        lax.fori_loop(0, n_r // 16, widen, 0)

    def wait_fast(slab):
        def wait(j, _):
            fast_copy(slab, j).wait_recv()
            return 0

        lax.fori_loop(0, HALF, wait, 0)

    def load_and_smooth(slab, i):
        for part in range(3):

            @pl.when(i == cuts[part])
            def _():
                load(part, slab).wait()
                wait_rows(part, slab)

        smooth(slab, slow_frame(i), jnp.minimum(i, HALF))

        @pl.when(jnp.logical_and(i < HALF, has_slow))
        def _():
            slow_copy(slab, i).start()

        @pl.when(i >= n_frame - HALF)
        def _():
            fast_copy(slab, n_frame - 1 - i).start()

    def first_slab(i, _):
        load_and_smooth(1, i)
        return 0

    wait_strips(1)
    lax.fori_loop(0, n_frame, first_slab, 0)
    rest = n_frame - HALF

    def filter_frame(slab, f):
        scale = inverse[f]
        for row in range(0, n_r, 8):
            for tile in range(tiles):
                where = (slice(row, row + 8), slice(tile * LANES, (tile + 1) * LANES))
                total = taps[0] * ext[slab][(f,) + where]
                for t in range(1, TAPS):
                    total = total + taps[t] * ext[slab][(f + t,) + where]
                own[slab][(f,) + where] = (ext[slab][(f + HALF,) + where] - total * scale).astype(BF16)

    def filter_slab(slab, start, stop):
        def step(i, _):
            @pl.when(jnp.logical_and(i >= rest, has_slow))
            def _():
                arrive(slab, i - rest)

            filter_frame(slab, slow_frame(jnp.where(i < rest, HALF + i, n_frame - 1 - i)))
            return 0

        lax.fori_loop(start, stop, step, 0)

    def second_slab(i, _):
        load_and_smooth(0, i)
        return 0

    wait_strips(0)
    lax.fori_loop(0, n_frame, second_slab, 0)
    wait_fast(1)
    filter_slab(1, 0, rest)
    wait_fast(0)
    filter_slab(0, 0, rest)
    filter_slab(1, rest, n_frame)

    normalize_patches(own[1], spots, counts, 1, windows, patches, normed, False)
    mirror_copy = pltpu.make_async_remote_copy(
        src_ref=normed,
        dst_ref=mirror,
        send_sem=mirror_send,
        recv_sem=mirror_recv,
        device_id=at(row=n_row - 1 - r, col=1 - c),
        device_id_type=MESH,
    )
    mirror_copy.start()
    filter_slab(0, rest, n_frame)

    mirror_copy.wait()
    for slab in (1, 0):
        each_strip(slab, lambda copy: copy.wait_send())
    for slab in (1, 0):
        for part in range(3):

            @pl.when(has_up)
            def _():
                rows_copy(part, slab, 0).wait_send()

            @pl.when(has_down)
            def _():
                rows_copy(part, slab, 1).wait_send()

        def finish(j, _):
            fast_copy(slab, j).wait_send()

            @pl.when(has_slow)
            def _():
                slow_copy(slab, j).wait_send()

            return 0

        lax.fori_loop(0, HALF, finish, 0)


def layer(sizes, frames, omega_taps, smooth_kernel, spots, counts):
    n_omega, n_row, n_frame, n_r, n_c = sizes
    tiles = n_c // LANES
    n_slot = spots.shape[2]
    hbm = pl.BlockSpec(memory_space=pl.ANY)
    smem = pl.BlockSpec(memory_space=pltpu.SMEM)
    vmem = pl.BlockSpec(memory_space=pltpu.VMEM)
    dma = pltpu.SemaphoreType.DMA
    return pl.pallas_call(
        functools.partial(layer_kernel, sizes),
        out_shape=(
            pltpu.VMEM(frames.shape[1:], BF16),
            pltpu.VMEM(frames.shape[1:], BF16),
            pltpu.VMEM((n_slot, PATCH * PATCH), BF16),
        ),
        in_specs=[hbm, smem, smem, smem, smem],
        out_specs=(vmem, vmem, vmem),
        scratch_shapes=[
            pltpu.VMEM((n_frame + 2 * HALF, n_r, n_c), F32),
            pltpu.VMEM((n_frame + 2 * HALF, n_r, n_c), F32),
            pltpu.VMEM((2, HALF + 1, n_r, n_c), BF16),
            pltpu.VMEM((2, HALF, n_r, n_c), BF16),
            pltpu.VMEM((2, n_frame, 16, n_c), BF16),
            pltpu.VMEM((2, n_frame, n_r, LANES), BF16),
            pltpu.VMEM((2, n_r, LANES), BF16),
            pltpu.VMEM((2, n_r + 16, LANES), BF16),
            pltpu.VMEM((n_r + 16, LANES), BF16),
            pltpu.VMEM((2, 5 * n_r // 2, 2 * (n_r // 2 + 32)), BF16),
            pltpu.VMEM((5 * n_r // 2, n_c + LANES), F32),
            pltpu.VMEM((5 * n_r // 2, n_c + LANES), F32),
            pltpu.VMEM((n_frame, 8, LANES), F32),
            dma((3, 2)),
            dma((2,)),
            dma((2, 3, 2)),
            dma((2, 3, 2)),
            dma((3, 2)),
            dma((3, 2)),
            dma((2, HALF)),
            dma((2, HALF)),
            dma((2, HALF)),
            dma((2, HALF)),
            pltpu.VMEM((8 * 24, LANES), F32),
            pltpu.VMEM((n_slot * PATCH, LANES), F32),
            pltpu.VMEM((n_slot, PATCH * PATCH), BF16),
            dma,
            dma,
        ],
        compiler_params=pltpu.CompilerParams(
            collective_id=0, has_side_effects=True, vmem_limit_bytes=54 * 1024 * 1024
        ),
        name="layer",
    )(frames, omega_taps, smooth_kernel, spots, counts)


def score_kernel(
    held_0, held_1, mirror, spots, counts, out, scores, windows, patches, normed, out_sem
):
    def put(slab):
        return pltpu.make_async_copy((held_0, held_1)[slab], out.at[slab], out_sem.at[slab])

    for slab in (0, 1):
        put(slab).start()
    normalize_patches(held_0, spots, counts, 0, windows, patches, normed, True)
    scores[...] = (
        lax.dot_general(
            normed[...], mirror[...], (((1,), (1,)), ((), ())), preferred_element_type=F32
        )
        / 256.0
    )
    for slab in (0, 1):
        put(slab).wait()


def score(raw, spots, counts, mirror):
    n_slot = mirror.shape[0]
    hbm = pl.BlockSpec(memory_space=pl.ANY)
    smem = pl.BlockSpec(memory_space=pltpu.SMEM)
    vmem = pl.BlockSpec(memory_space=pltpu.VMEM)
    held = [pltpu.with_memory_space_constraint(x, pltpu.VMEM) for x in (*raw, mirror)]
    return pl.pallas_call(
        score_kernel,
        out_shape=(
            jax.ShapeDtypeStruct((2,) + raw[0].shape, BF16),
            jax.ShapeDtypeStruct((n_slot, n_slot), F32),
        ),
        in_specs=[vmem, vmem, vmem, smem, smem],
        out_specs=(hbm, vmem),
        scratch_shapes=[
            pltpu.VMEM((8 * 24, LANES), F32),
            pltpu.VMEM((n_slot * PATCH, LANES), F32),
            pltpu.VMEM((n_slot, PATCH * PATCH), BF16),
            pltpu.SemaphoreType.DMA((2,)),
        ],
        compiler_params=pltpu.CompilerParams(vmem_limit_bytes=16 * 1024 * 1024),
        name="score",
    )(*held, spots, counts)


def solution(mesh):
    n_omega, n_row = (mesh.shape[axis] for axis in ("omega", "row"))

    def shards(frames, omega_taps, smooth_kernel, spots, counts):
        sizes = (n_omega, n_row) + frames.shape[1:]
        spots = jnp.transpose(spots, (1, 0, 2))
        counts = jnp.transpose(counts, (1, 0))
        *raw, mirror = layer(sizes, frames, omega_taps, smooth_kernel, spots, counts)
        smoothed, scores = score(raw, spots, counts, mirror)
        return (smoothed, scores)

    return jax.shard_map(
        shards,
        mesh=mesh,
        in_specs=(
            P(None, "omega", "row", "col"),
            P(),
            P(),
            P(None, None, ("omega", "row", "col")),
            P(None, ("omega", "row", "col")),
        ),
        out_specs=(P(None, "omega", "row", "col"), P(("omega", "row", "col"), None)),
        check_vma=False,
    )
```

profile of v0, /device:TPU:39, one launch (start us, length us, event | category | flops | bytes accessed | tf_op | source)
XLA Modules:
  0.0 98.3 jit_solution(11090289310885228440)
XLA Ops:
  0.6 0.0 copy-start.1
  0.6 0.0 copy-start
  0.7 93.0 %layer.1 = (bf16[16,128,1024]{2,1,0:T(8,128)(2,1)S(1)}, bf16[16,128,1024]{2,1,0:T(8,128)(2,1)S(1)}, bf16[128,256]{1,0:T(8,128)(2,1)S(1)}) custom-call(bf16[2,16,128,1024]{3,2,1,0:T(8,128)(2,1)} %frames.1, f32[15]{0:T(128)} %taps.1, f32[5,5]{1,0:T(8,128)} %weights.1, s32[3,2,128]{2,1,0:T(2,128)} %bitcast.2, s32[1,2]{1,0:T(1,128)} %bitcast.4), custom_call_target="tpu_custom_call" | custom-call | tf_op jit(solution)/shard_map/layer/pallas_call | solution.py:532
  93.7 0.0 copy-done.1
  93.7 0.0 copy-done
  93.7 4.6 %score.1 = (bf16[2,16,128,1024]{3,2,1,0:T(8,128)(2,1)}, f32[128,128]{1,0:T(8,128)}) custom-call(bf16[16,128,1024]{2,1,0:T(8,128)(2,1)S(1)} %get-tuple-element.5.held_0, bf16[16,128,1024]{2,1,0:T(8,128)(2,1)S(1)} %get-tuple-element.6.held_1, bf16[128,256]{1,0:T(8,128)(2,1)S(1)} %get-tuple-element.7.mirror, s32[3,2,128]{2,1,0:T(2,128)S(1)} %bitcast.3, ...), custom_call_target="tpu_custom_call" | custom-call | tf_op jit(solution)/shard_map/score/pallas_call | solution.py:603
Async XLA Ops:
  0.6 93.1 %copy-start.1 = (s32[2,1]{0,1:T(1,128)S(1)}, s32[2,1]{0,1:T(1,128)}, u32[]{:S(2)}) copy-start(s32[2,1]{0,1:T(1,128)} %param.9) | copy-start | bytes 28
  0.6 93.1 %copy-start = (s32[2,3,128]{2,0,1:T(2,128)S(1)}, s32[2,3,128]{2,0,1:T(2,128)}, u32[]{:S(2)}) copy-start(s32[2,3,128]{2,0,1:T(2,128)} %param.8) | copy-start | bytes 9220
where the time goes:
time: 100 us; the launch traced here: 98.3 us
  Pallas kernels  97.6 us (98%)
    pallas_call x1, Pallas kernels, layer(): pl.pallas_call(functools.partial(layer_kernel, sizes), out_shape=(pltpu.V...  93 us
    pallas_call x1, Pallas kernels, score(): pl.pallas_call(score_kernel, out_shape=(jax.ShapeDtypeStruct((2,) + raw[0...  4.63 us

commit v1 on v0

--- a/solution.py
+++ b/solution.py
@@ -45,12 +45,12 @@
                 moved_right = pltpu.roll(right, LANES - bit, 1)
                 left = jnp.where(on, jnp.where(lane < LANES - bit, moved_left, moved_right), left)
                 right = jnp.where(on, moved_right, right)
-        at_window = (i & 7) * 24
+        at_window = (i & 15) * 24
         windows[pl.ds(at_window, 24)] = left
         patches[pl.ds(i * PATCH, PATCH)] = windows[pl.ds(at_window + (row - row_0), PATCH)]
         return 0
 
-    lax.fori_loop(0, n_slot, one, 0, unroll=8)
+    lax.fori_loop(0, n_slot, one, 0, unroll=16)
     halves = []
     for half in range(2):
         total = jnp.zeros((n_slot, LANES), F32)
@@ -493,9 +493,6 @@
         device_id_type=MESH,
     )
     mirror_copy.start()
-    filter_slab(0, rest, n_frame)
-
-    mirror_copy.wait()
     for slab in (1, 0):
         each_strip(slab, lambda copy: copy.wait_send())
     for slab in (1, 0):
@@ -511,14 +508,21 @@
 
         def finish(j, _):
             fast_copy(slab, j).wait_send()
-
-            @pl.when(has_slow)
-            def _():
+            return 0
+
+        lax.fori_loop(0, HALF, finish, 0)
+
+    filter_slab(0, rest, n_frame)
+
+    mirror_copy.wait()
+    @pl.when(has_slow)
+    def _():
+        def sent(j, _):
+            for slab in (1, 0):
                 slow_copy(slab, j).wait_send()
-
             return 0
 
-        lax.fori_loop(0, HALF, finish, 0)
+        lax.fori_loop(0, HALF, sent, 0)
 
 
 def layer(sizes, frames, omega_taps, smooth_kernel, spots, counts):
@@ -562,7 +566,7 @@
             dma((2, HALF)),
             dma((2, HALF)),
             dma((2, HALF)),
-            pltpu.VMEM((8 * 24, LANES), F32),
+            pltpu.VMEM((16 * 24, LANES), F32),
             pltpu.VMEM((n_slot * PATCH, LANES), F32),
             pltpu.VMEM((n_slot, PATCH * PATCH), BF16),
             dma,
@@ -609,7 +613,7 @@
         in_specs=[vmem, vmem, vmem, smem, smem],
         out_specs=(hbm, vmem),
         scratch_shapes=[
-            pltpu.VMEM((8 * 24, LANES), F32),
+            pltpu.VMEM((16 * 24, LANES), F32),
             pltpu.VMEM((n_slot * PATCH, LANES), F32),
             pltpu.VMEM((n_slot, PATCH * PATCH), BF16),
             pltpu.SemaphoreType.DMA((2,)),

time: 100 us -> 100 us (level)
  no operation moved by 1% of the time
where the time goes in v1:
time: 100 us; the launch traced here: 98.2 us
  Pallas kernels  97.5 us (98%)
    pallas_call x1, Pallas kernels, layer(): pl.pallas_call(functools.partial(layer_kernel, sizes), out_shape=(pltpu.V...  92.9 us
    pallas_call x1, Pallas kernels, score(): pl.pallas_call(score_kernel, out_shape=(jax.ShapeDtypeStruct((2,) + raw[0...  4.63 us

profile of v1, /device:TPU:39, one launch (start us, length us, event | category | flops | bytes accessed | tf_op | source)
XLA Modules:
  0.0 98.2 jit_solution(4615294813752808722)
XLA Ops:
  0.6 0.0 copy-start.1
  0.6 0.0 copy-start
  0.7 92.9 %layer.1 = (bf16[16,128,1024]{2,1,0:T(8,128)(2,1)S(1)}, bf16[16,128,1024]{2,1,0:T(8,128)(2,1)S(1)}, bf16[128,256]{1,0:T(8,128)(2,1)S(1)}) custom-call(bf16[2,16,128,1024]{3,2,1,0:T(8,128)(2,1)} %frames.1, f32[15]{0:T(128)} %taps.1, f32[5,5]{1,0:T(8,128)} %weights.1, s32[3,2,128]{2,1,0:T(2,128)} %bitcast.2, s32[1,2]{1,0:T(1,128)} %bitcast.4), custom_call_target="tpu_custom_call" | custom-call | tf_op jit(solution)/shard_map/layer/pallas_call | solution.py:536
  93.6 0.0 copy-done.1
  93.6 0.0 copy-done
  93.6 4.6 %score.1 = (bf16[2,16,128,1024]{3,2,1,0:T(8,128)(2,1)}, f32[128,128]{1,0:T(8,128)}) custom-call(bf16[16,128,1024]{2,1,0:T(8,128)(2,1)S(1)} %get-tuple-element.5.held_0, bf16[16,128,1024]{2,1,0:T(8,128)(2,1)S(1)} %get-tuple-element.6.held_1, bf16[128,256]{1,0:T(8,128)(2,1)S(1)} %get-tuple-element.7.mirror, s32[3,2,128]{2,1,0:T(2,128)S(1)} %bitcast.3, ...), custom_call_target="tpu_custom_call" | custom-call | tf_op jit(solution)/shard_map/score/pallas_call | solution.py:607
Async XLA Ops:
  0.6 92.9 %copy-start.1 = (s32[2,1]{0,1:T(1,128)S(1)}, s32[2,1]{0,1:T(1,128)}, u32[]{:S(2)}) copy-start(s32[2,1]{0,1:T(1,128)} %param.9) | copy-start | bytes 28
  0.6 92.9 %copy-start = (s32[2,3,128]{2,0,1:T(2,128)S(1)}, s32[2,3,128]{2,0,1:T(2,128)}, u32[]{:S(2)}) copy-start(s32[2,3,128]{2,0,1:T(2,128)} %param.8) | copy-start | bytes 9220
